TPU v7x, 32 devices: a whole 2x2x4 slice. The times are simulated.
32 devices in a mesh: groups: 2 (over y), dp: 4 (over z), tensor: 2 (over x), layer: 2 (over core).
Axes of the slice: x: 2, y: 2, z: 4, core: 2. Of those that a mesh axis runs over, the one named last changes fastest.
Arguments:
- train_inputs: bfloat16 [2, 256, 16, 8192], P('layer', ('groups', 'dp'), None, 'tensor'), parts along dimension 1, may hold values from -6 to 6
- train_grads: bfloat16 [2, 256, 16, 8192], P('layer', ('groups', 'dp'), None, 'tensor'), parts along dimension 1, may hold values from -6 to 6
- bench_inputs: bfloat16 [2, 128, 16, 8192], P('layer', ('groups', 'dp'), None, 'tensor'), parts along dimension 1, may hold values from -6 to 6
- bench_grads: bfloat16 [2, 128, 16, 8192], P('layer', ('groups', 'dp'), None, 'tensor'), parts along dimension 1, may hold values from -6 to 6
- answer_mask: int32 [128, 16], P(('groups', 'dp')), parts along dimension 0, may hold values 0 or 1
- factors: bfloat16 [2, 8192, 128], P('layer', 'tensor'), may hold values from -0.0625 to 0.0625
- precond: bfloat16 [2, 4096, 4096], P('layer', None, ('dp', 'tensor')), may hold values from -0.09375 to 0.09375
Outputs:
- scores: float32 [256, 64], P(('groups', 'dp', 'tensor', 'layer')), parts along dimension 0
There are 2 independent parts, one for each index of `groups`. A program takes and returns all parts, laid end to end along the dimension named above; an argument that names none is the same for every part. Nothing has to cross between parts.
All inputs are finite; a program needn't handle non-finite values. No bound on the sum of `answer_mask` on one device may be relied on, other than what follows from the above.
Results may differ from a plain program's by a relative error of at most 0.005.
Values may be sent and summed in bfloat16 or wider, within the bound.
A program may use at most 64 MiB of HBM per device.

v0:
```python
import math
import jax
import jax.numpy as jnp
from jax import lax
from jax.sharding import PartitionSpec as P


def project(inputs_here, grads_here, factor):
    examples, length, shard_width = inputs_here.shape
    factor_width = factor.shape[1] // 2
    in_proj = jnp.dot(
        inputs_here.reshape(examples * length, shard_width),
        factor[:, :factor_width],
        preferred_element_type=jnp.float32,
    )
    out_proj = jnp.dot(
        grads_here.reshape(examples * length, shard_width),
        factor[:, factor_width:],
        preferred_element_type=jnp.float32,
    )
    return jnp.concatenate([in_proj, out_proj], axis=1)


def outer_features(token_rows, examples, length, factor_width):
    grouped = token_rows.reshape(examples, length, 2 * factor_width)
    outer = jnp.einsum(
        "esa,esb->eab",
        grouped[..., factor_width:],
        grouped[..., :factor_width],
        precision=lax.Precision.HIGHEST,
    ) / math.sqrt(length)
    return outer.reshape(examples, factor_width * factor_width).astype(jnp.bfloat16)


def local(train_inputs, train_grads, bench_inputs, bench_grads, answer_mask, factors, precond):
    factor = factors[0]
    factor_width = factor.shape[1] // 2
    length = train_inputs.shape[2]
    masked = bench_grads[0] * answer_mask.astype(jnp.bfloat16)[:, :, None]
    train_rows = project(train_inputs[0], train_grads[0], factor)
    bench_rows = project(bench_inputs[0], masked, factor)
    tensor_count = lax.axis_size("tensor")
    train_each = train_inputs.shape[1] // tensor_count
    bench_each = bench_inputs.shape[1] // tensor_count
    row_width = train_rows.shape[1]
    blocks = jnp.concatenate(
        [
            train_rows.reshape(tensor_count, train_each * length, row_width),
            bench_rows.reshape(tensor_count, bench_each * length, row_width),
        ],
        axis=1,
    ).reshape(-1, row_width)
    share_rows = blocks.shape[0] // tensor_count
    summed = lax.psum(blocks, "tensor")
    own_rows = lax.dynamic_slice_in_dim(
        summed, lax.axis_index("tensor") * share_rows, share_rows, 0
    )
    train_feats = outer_features(own_rows[: train_each * length], train_each, length, factor_width)
    bench_feats = outer_features(own_rows[train_each * length :], bench_each, length, factor_width)
    columns = precond[0]
    pre_cols = jnp.dot(
        lax.all_gather(bench_feats, ("dp", "tensor"), axis=0, tiled=True),
        columns,
        preferred_element_type=jnp.float32,
    ).astype(jnp.bfloat16)
    layer_total = lax.axis_size("layer") * train_inputs.shape[0]
    score_scale = 1.0 / math.sqrt(factor_width * factor_width * layer_total)
    whole_pre = lax.all_gather(pre_cols, ("dp", "tensor"), axis=1, tiled=True)
    partial_value = jnp.einsum(
        "ek,jk->ej", train_feats, whole_pre, preferred_element_type=jnp.float32
    )
    scores = lax.psum_scatter(partial_value, "layer", scatter_dimension=0, tiled=True)
    return scores * score_scale


def solution(mesh):
    placed = (
        P("layer", ("groups", "dp"), None, "tensor"),
        P("layer", ("groups", "dp"), None, "tensor"),
        P("layer", ("groups", "dp"), None, "tensor"),
        P("layer", ("groups", "dp"), None, "tensor"),
        P(("groups", "dp"), None),
        P("layer", "tensor", None),
        P("layer", None, ("dp", "tensor")),
    )
    return jax.shard_map(
        local,
        mesh=mesh,
        in_specs=placed,
        out_specs=P(("groups", "dp", "tensor", "layer"), None),
        check_vma=False,
    )
```

profile of v0, /device:TPU:0, one launch (start us, length us, event | category | flops | bytes accessed | tf_op | source)
XLA Modules:
  0.0 126.8 jit_solution(3071101061029327510)
XLA Ops:
  6.5 0.0 copy-start
  6.5 0.0 copy-start.1
  6.5 0.0 all-reduce.3.cloned.1.call-start
  6.5 0.9 convert_element_type.18
  7.4 0.1 mul.20
  7.5 1.8 %bitcast_multiply_fusion = bf16[256,4096]{1,0:T(8,128)(2,1)S(1)} fusion(bf16[1,16,16,4096]{3,2,1,0:T(8,128)(2,1)} %param.10, bf16[256]{0:T(256)(128)(2,1)S(1)} %mul.20), kind=kLoop, calls=%fused_computation.2 | loop fusion | flops 1048576 | bytes 4194816 | tf_op jit(solution)/shard_map/mul | solution.py:39
  9.3 0.0 copy-done.1
  9.3 1.3 %fusion.7 = f32[256,64]{0,1:T(8,128)S(1)} fusion(bf16[256,4096]{1,0:T(8,128)(2,1)S(1)} %bitcast_multiply_fusion, bf16[4096,128]{1,0:T(8,128)(2,1)S(1)} %bitcast.27), kind=kOutput, calls=%fused_computation.8 | convolution fusion | flops 134217728 | bytes 3211264 | tf_op jit(solution)/shard_map/dot_general | solution.py:16
  10.7 0.0 copy-done
  10.7 0.8 fusion.11
  11.5 0.1 reshape.25
  11.6 0.0 copy-start.2
  11.6 3.7 %fusion.13 = f32[512,64]{0,1:T(8,128)S(1)} fusion(bf16[512,4096]{1,0:T(8,128)(2,1)} %bitcast.31, bf16[4096,128]{1,0:T(8,128)(2,1)S(1)} %bitcast.29), kind=kOutput, calls=%fused_computation.14 | convolution fusion | flops 268435456 | bytes 5373952 | tf_op jit(solution)/shard_map/dot_general | solution.py:11
  15.3 0.0 copy-done.2
  15.3 0.0 copy-start.3
  15.3 1.7 %fusion.9 = f32[512,64]{0,1:T(8,128)S(1)} fusion(bf16[512,4096]{1,0:T(8,128)(2,1)S(1)} %bitcast.32, bf16[4096,128]{1,0:T(8,128)(2,1)S(1)} %bitcast.30), kind=kOutput, calls=%fused_computation.10 | convolution fusion | flops 268435456 | bytes 5373952 | tf_op jit(solution)/shard_map/dot_general | solution.py:16
  17.1 0.2 reshape.24
  17.3 0.2 pad_maximum_fusion
  17.4 0.9 copy.10
  18.4 0.0 all-reduce.3.cloned.1.call-update
  18.4 0.0 copy-done.3
  18.4 0.6 dynamic-slice
  19.7 27.3 %all-reduce.3.cloned.1.call-done = f32[768,128]{1,0:T(8,128)} async-done(((f32[768,128]{1,0:T(8,128)}), f32[768,128]{1,0:T(8,128)}) %all-reduce.3.cloned.1.call-update) | async-done | bytes 393232 | tf_op jit(solution)/shard_map/psum | solution.py:54
  47.0 0.8 constant_dynamic-slice_fusion.1
  47.8 0.7 fusion.3
  48.5 0.2 convert_element_type.22
  48.7 31.4 %all_gather.6 = bf16[64,4096]{1,0:T(8,128)(2,1)S(1)} all-gather(bf16[8,4096]{1,0:T(8,128)(2,1)S(1)} %convert_element_type.22), channel_id=1, replica_groups=mesh['groups'=2,'dp'=4,'tensor'=2,'layer'=2] {'dp','tensor'}, dimensions={0}, use_global_device_ids=true | all-gather | bytes 589824 | tf_op jit(solution)/shard_map/all_gather | solution.py:62
  80.1 3.0 %fusion.4 = bf16[64,512]{1,0:T(8,128)(2,1)S(1)} fusion(bf16[64,4096]{1,0:T(8,128)(2,1)S(1)} %all_gather.6, bf16[1,4096,512]{2,1,0:T(8,128)(2,1)} %param.13), kind=kOutput, calls=%fused_computation.7 | convolution fusion | flops 268468224 | bytes 4784128 | tf_op jit(solution)/shard_map/dot_general | solution.py:61
  83.2 31.2 %all_gather.7 = bf16[64,4096]{1,0:T(8,128)(2,1)S(1)} all-gather(bf16[64,512]{1,0:T(8,128)(2,1)S(1)} %fusion.4), channel_id=1, replica_groups=mesh['groups'=2,'dp'=4,'tensor'=2,'layer'=2] {'dp','tensor'}, dimensions={1}, use_global_device_ids=true | all-gather | bytes 589824 | tf_op jit(solution)/shard_map/all_gather | solution.py:68
  114.4 0.9 constant_dynamic-slice_fusion
  115.3 1.1 fusion.2
  116.4 0.3 convert_element_type.20
  116.7 0.2 fusion.19
  116.9 2.5 %all-reduce = f32[16,64]{1,0:T(8,128)S(1)} all-reduce(f32[16,64]{1,0:T(8,128)S(1)} %fusion.19), channel_id=2, replica_groups=mesh['groups'=2,'dp'=4,'tensor'=2,'layer'=2] {'layer'}, use_global_device_ids=true, to_apply=%region_1.0.clone | all-reduce | flops 1024 | bytes 8192
  119.4 0.6 dynamic-slice_multiply_fusion
  (2 shorter events, 0.0 us)
Async XLA Ops:
  6.5 4.2 %copy-start = (bf16[1,16,16,4096]{3,2,1,0:T(8,128)(2,1)S(1)}, bf16[1,16,16,4096]{3,2,1,0:T(8,128)(2,1)}, u32[]{:S(2)}) copy-start(bf16[1,16,16,4096]{3,2,1,0:T(8,128)(2,1)} %param.9) | copy-start | bytes 6291460
  6.5 2.8 %copy-start.1 = (bf16[1,4096,128]{2,1,0:T(8,128)(2,1)S(1)}, bf16[1,4096,128]{2,1,0:T(8,128)(2,1)}, u32[]{:S(2)}) copy-start(bf16[1,4096,128]{2,1,0:T(8,128)(2,1)} %param.12) | copy-start | bytes 3145732
  6.5 40.5 %all-reduce.3.cloned.1.call-start = ((), (), s32[]{:S(2)}) async-start(), calls=%async_computation | async-start | bytes 786432 | tf_op jit(solution)/shard_map/psum | solution.py:54
  11.6 3.7 %copy-start.2 = (bf16[1,32,16,4096]{3,2,1,0:T(8,128)(2,1)S(1)}, bf16[1,32,16,4096]{3,2,1,0:T(8,128)(2,1)}, u32[]{:S(2)}) copy-start(bf16[1,32,16,4096]{3,2,1,0:T(8,128)(2,1)} %param.8) | copy-start | bytes 12582916
  15.3 3.1 %copy-start.3 = (u32[32]{0:T(128)S(1)}, u32[32]{0:T(128)}, u32[]{:S(2)}) copy-start(u32[32]{0:T(128)} %constant.25) | copy-start | bytes 388
Sparse Core Ops, SparseCore 0:
  18.5 28.4 all-reduce.2
where the time goes:
time: 127 us
  blocking collectives  65.1 us (51%)
  waiting for transfers between devices  27.3 us (21%)
  between operations  14.2 us (11%)
  matrix products  12.6 us (10%)
  local copies, waits for them, and re-layouts  4.08 us (3%)
  other arithmetic  3.48 us (3%)
    all_gather x1, blocking collectives, local(): lax.all_gather(bench_feats, ('dp', 'tensor'), axis=0, tiled=True)  31.4 us
    all_gather x1, blocking collectives, local(): whole_pre = lax.all_gather(pre_cols, ('dp', 'tensor'), axis=1, tiled=True)  31.2 us
    psum x1, waiting for transfers between devices, local(): summed = lax.psum(blocks, 'tensor')  27.3 us
    dot_general x2, matrix products, project(): jnp.dot(inputs_here.reshape(examples * length, shard_width), factor[:, :f...  4.5 us
    dot_general x2, matrix products, project(): jnp.dot(grads_here.reshape(examples * length, shard_width), factor[:, fac...  3.09 us
    dot_general x1, matrix products, local(): jnp.dot(lax.all_gather(bench_feats, ('dp', 'tensor'), axis=0, tiled=True)...  3.02 us
  transfers between devices with their start and end apart: 1, of which 1 were waited for; matrix products, arithmetic and copies ran while one was open for 0% of the time, Pallas kernels for 0%

commit v1 on v0

--- a/solution.py
+++ b/solution.py
@@ -51,7 +51,7 @@
         axis=1,
     ).reshape(-1, row_width)
     share_rows = blocks.shape[0] // tensor_count
-    summed = lax.psum(blocks, "tensor")
+    summed = jnp.sum(lax.all_gather(blocks, "tensor"), axis=0)
     own_rows = lax.dynamic_slice_in_dim(
         summed, lax.axis_index("tensor") * share_rows, share_rows, 0
     )

time: 127 us -> 97.2 us (0.77)
  waiting for transfers between devices: 27.3 us -> 0 us
  between operations: 14.2 us -> 0.81 us
  blocking collectives: 65.1 us -> 78.4 us
  local copies, waits for them, and re-layouts: 4.08 us -> 1.6 us
    psum x1 -> x0, waiting for transfers between devices: 27.3 us -> none  [local(): summed = lax.psum(blocks, 'tensor')]
    all_gather x0 -> x1, blocking collectives: none -> 12.7 us  [local(): summed = jnp.sum(lax.all_gather(blocks, 'tensor'), axis=0)]
  transfers between devices with their start and end apart: 1 -> 0, of which waited for: 1 -> 0; matrix products, arithmetic and copies ran while one was open for 0% -> 0% of each run, Pallas kernels for 0% -> 0%
where the time goes in v1:
time: 97.2 us; the launch traced here: 96.9 us
  blocking collectives  78.4 us (81%)
  matrix products  12.6 us (13%)
  other arithmetic  3.54 us (4%)
  local copies, waits for them, and re-layouts  1.6 us (2%)
    all_gather x1, blocking collectives, local(): lax.all_gather(bench_feats, ('dp', 'tensor'), axis=0, tiled=True)  31.9 us
    all_gather x1, blocking collectives, local(): whole_pre = lax.all_gather(pre_cols, ('dp', 'tensor'), axis=1, tiled=True)  31.2 us
    all_gather x1, blocking collectives, local(): summed = jnp.sum(lax.all_gather(blocks, 'tensor'), axis=0)  12.7 us
    dot_general x2, matrix products, project(): jnp.dot(inputs_here.reshape(examples * length, shard_width), factor[:, :f...  4.5 us
    dot_general x2, matrix products, project(): jnp.dot(grads_here.reshape(examples * length, shard_width), factor[:, fac...  3.09 us
    dot_general x1, matrix products, local(): jnp.dot(lax.all_gather(bench_feats, ('dp', 'tensor'), axis=0, tiled=True)...  3.02 us
    unnamed x1, blocking collectives  2.48 us

profile of v1, /device:TPU:0, one launch (start us, length us, event | category | flops | bytes accessed | tf_op | source)
XLA Modules:
  0.0 96.9 jit_solution(14194496419898839394)
XLA Ops:
  0.0 0.0 copy-start
  0.0 0.0 copy-start.1
  0.0 0.9 convert_element_type.18
  0.9 0.1 mul.20
  1.0 1.8 %bitcast_multiply_fusion = bf16[256,4096]{1,0:T(8,128)(2,1)S(1)} fusion(bf16[1,16,16,4096]{3,2,1,0:T(8,128)(2,1)} %param.10, bf16[256]{0:T(256)(128)(2,1)S(1)} %mul.20), kind=kLoop, calls=%fused_computation.2 | loop fusion | flops 1048576 | bytes 4194816 | tf_op jit(solution)/shard_map/mul | solution.py:39
  2.8 0.0 copy-done.1
  2.8 1.3 %fusion.7 = f32[256,64]{0,1:T(8,128)S(1)} fusion(bf16[256,4096]{1,0:T(8,128)(2,1)S(1)} %bitcast_multiply_fusion, bf16[4096,128]{1,0:T(8,128)(2,1)S(1)} %bitcast.27), kind=kOutput, calls=%fused_computation.8 | convolution fusion | flops 134217728 | bytes 3211264 | tf_op jit(solution)/shard_map/dot_general | solution.py:16
  4.2 0.0 copy-done
  4.2 0.8 fusion.11
  4.9 0.1 reshape.22
  5.0 0.0 copy-start.2
  5.0 3.7 %fusion.13 = f32[512,64]{0,1:T(8,128)S(1)} fusion(bf16[512,4096]{1,0:T(8,128)(2,1)} %bitcast.31, bf16[4096,128]{1,0:T(8,128)(2,1)S(1)} %bitcast.29), kind=kOutput, calls=%fused_computation.14 | convolution fusion | flops 268435456 | bytes 5373952 | tf_op jit(solution)/shard_map/dot_general | solution.py:11
  8.8 0.0 copy-done.2
  8.8 1.7 %fusion.9 = f32[512,64]{0,1:T(8,128)S(1)} fusion(bf16[512,4096]{1,0:T(8,128)(2,1)S(1)} %bitcast.32, bf16[4096,128]{1,0:T(8,128)(2,1)S(1)} %bitcast.30), kind=kOutput, calls=%fused_computation.10 | convolution fusion | flops 268435456 | bytes 5373952 | tf_op jit(solution)/shard_map/dot_general | solution.py:16
  10.5 0.2 reshape.21
  10.7 0.2 pad_maximum_fusion
  10.9 0.2 copy.8
  11.1 12.7 %all_gather.9 = f32[2,768,128]{2,1,0:T(8,128)S(1)} all-gather(f32[1,768,128]{2,1,0:T(8,128)S(1)} %bitcast.33), channel_id=1, replica_groups=mesh['groups'=2,'dp'=4,'tensor'=2,'layer'=2] {'tensor'}, dimensions={0}, use_global_device_ids=true | all-gather | bytes 1179648 | tf_op jit(solution)/shard_map/all_gather | solution.py:54
  23.8 0.1 reduce_sum.9
  23.9 0.0 copy-start.3
  23.9 0.7 fusion.3
  24.6 0.2 convert_element_type.22
  24.8 31.9 %all_gather.10 = bf16[64,4096]{1,0:T(8,128)(2,1)S(1)} all-gather(bf16[8,4096]{1,0:T(8,128)(2,1)S(1)} %convert_element_type.22), channel_id=1, replica_groups=mesh['groups'=2,'dp'=4,'tensor'=2,'layer'=2] {'dp','tensor'}, dimensions={0}, use_global_device_ids=true | all-gather | bytes 589824 | tf_op jit(solution)/shard_map/all_gather | solution.py:62
  56.7 3.0 %fusion.4 = bf16[64,512]{1,0:T(8,128)(2,1)S(1)} fusion(bf16[64,4096]{1,0:T(8,128)(2,1)S(1)} %all_gather.10, bf16[1,4096,512]{2,1,0:T(8,128)(2,1)} %param.13), kind=kOutput, calls=%fused_computation.7 | convolution fusion | flops 268468224 | bytes 4784128 | tf_op jit(solution)/shard_map/dot_general | solution.py:61
  59.8 31.2 %all_gather.11 = bf16[64,4096]{1,0:T(8,128)(2,1)S(1)} all-gather(bf16[64,512]{1,0:T(8,128)(2,1)S(1)} %fusion.4), channel_id=1, replica_groups=mesh['groups'=2,'dp'=4,'tensor'=2,'layer'=2] {'dp','tensor'}, dimensions={1}, use_global_device_ids=true | all-gather | bytes 589824 | tf_op jit(solution)/shard_map/all_gather | solution.py:68
  91.0 1.1 %fusion.2 = bf16[16,64,64]{2,1,0:T(8,128)(2,1)S(1)} fusion(f32[16,16,128]{2,1,0:T(8,128)S(1)} %bitcast.34), kind=kOutput, calls=%fused_computation.4 | convolution fusion | flops 12713984 | bytes 393216 | tf_op jit(solution)/shard_map/esa,esb->eab/dot_general | solution.py:26
  92.1 0.3 convert_element_type.20
  92.4 0.2 fusion.19
  92.6 2.5 %all-reduce = f32[16,64]{1,0:T(8,128)S(1)} all-reduce(f32[16,64]{1,0:T(8,128)S(1)} %fusion.19), channel_id=2, replica_groups=mesh['groups'=2,'dp'=4,'tensor'=2,'layer'=2] {'layer'}, use_global_device_ids=true, to_apply=%region_1.0.clone | all-reduce | flops 1024 | bytes 8192
  95.1 0.0 copy-done.3
  95.1 0.6 dynamic-slice
  96.3 0.6 dynamic-slice_multiply_fusion
  (4 shorter events, 0.1 us)
Async XLA Ops:
  0.0 4.2 %copy-start = (bf16[1,16,16,4096]{3,2,1,0:T(8,128)(2,1)S(1)}, bf16[1,16,16,4096]{3,2,1,0:T(8,128)(2,1)}, u32[]{:S(2)}) copy-start(bf16[1,16,16,4096]{3,2,1,0:T(8,128)(2,1)} %param.9) | copy-start | bytes 6291460
  0.0 2.8 %copy-start.1 = (bf16[1,4096,128]{2,1,0:T(8,128)(2,1)S(1)}, bf16[1,4096,128]{2,1,0:T(8,128)(2,1)}, u32[]{:S(2)}) copy-start(bf16[1,4096,128]{2,1,0:T(8,128)(2,1)} %param.12) | copy-start | bytes 3145732
  5.0 3.7 %copy-start.2 = (bf16[1,32,16,4096]{3,2,1,0:T(8,128)(2,1)S(1)}, bf16[1,32,16,4096]{3,2,1,0:T(8,128)(2,1)}, u32[]{:S(2)}) copy-start(bf16[1,32,16,4096]{3,2,1,0:T(8,128)(2,1)} %param.8) | copy-start | bytes 12582916
  23.9 71.2 %copy-start.3 = (u32[32]{0:T(128)S(1)}, u32[32]{0:T(128)}, u32[]{:S(2)}) copy-start(u32[32]{0:T(128)} %constant.27) | copy-start | bytes 388
